TPU v7x, 32 devices: a whole 2x2x4 slice. The times are simulated.
32 devices in a mesh: ctx: 8 (over z, x), fsdp: 4 (over y, core).
Axes of the slice: x: 2, y: 2, z: 4, core: 2. Of those that a mesh axis runs over, the one named last changes fastest.
Arguments:
- layer_input: bfloat16 [4096, 1024], P(('ctx', 'fsdp')), may hold values from -40 to 40, as said below
- gain_attn: bfloat16 [1024], P('fsdp'), may hold values from 0.25 to 1.75
- w_qkv: bfloat16 [1024, 3072], P('fsdp'), may hold values from -1 to 1
- w_out: bfloat16 [1024, 1024], P('fsdp'), may hold values from -3.5 to 3.5
- gain_mlp: bfloat16 [1024], P('fsdp'), may hold values from 0.25 to 1.75
- w_in: bfloat16 [1024, 5248], P('fsdp'), may hold values from -0.1875 to 0.1875
- w_down: bfloat16 [2624, 1024], P('fsdp'), may hold values from -0.125 to 0.125
- cotangent: bfloat16 [4096, 1024], P(('ctx', 'fsdp')), may hold values from -36 to 36
Outputs:
- layer_output: bfloat16 [4096, 1024], P(('ctx', 'fsdp'))
- d_x: float32 [4096, 1024], P(('ctx', 'fsdp'))
- d_gain_attn: float32 [1024], P('fsdp')
- d_gain_mlp: float32 [1024], P('fsdp')
- d_w_qkv: float32 [1024, 3072], P('fsdp')
- d_w_out: float32 [1024, 1024], P('fsdp')
- d_w_in: float32 [1024, 5248], P('fsdp')
- d_w_down: float32 [2624, 1024], P('fsdp')
Inputs may be any that keep to these rules, and one draw needn't show every extreme that they name: `layer_input`: input activations with feature scales and token scales that differ.
All inputs are finite; a program needn't handle non-finite values.
Results may differ from a plain program's by a relative error of at most 0.019.
Values may be sent and summed in bfloat16 or wider, within the bound.
No kernel may reach another device: no remote copies, remote signals or barrier semaphores. Data moves between devices by JAX's collectives and lax.ppermute only.
A program may use at most 448 MiB of HBM per device.

v0:
```python
import math
import jax
import jax.numpy as jnp
from jax import lax
from jax.sharding import PartitionSpec as P

H = 16
HD = 64
EPS = 1e-05
THETA = 160000.0
SQRT_HALF = 0.7071067811865476
INV_SQRT_TAU = 0.3989422804014327


def layer_norm(values, gain):
    middle = jnp.mean(values, axis=-1, keepdims=True)
    centered = values - middle
    spread = jnp.mean(centered * centered, axis=-1, keepdims=True)
    inverse = lax.rsqrt(spread + EPS)
    normed = centered * inverse
    return (normed * gain, normed, inverse)


def norm_back(incoming, normed, inverse, gain):
    scaled = incoming * gain
    return inverse * (
        scaled
        - jnp.mean(scaled, axis=-1, keepdims=True)
        - normed * jnp.mean(scaled * normed, axis=-1, keepdims=True)
    )


def rope_tables(positions, width):
    half = width // 2
    freq = THETA ** (-(jnp.arange(half).astype(jnp.float32) * 2.0 / width))
    angle = positions[:, None] * freq[None, :]
    return (jnp.cos(angle), jnp.sin(angle))


def rotate(values, cosine, sine, sign):
    half = values.shape[-1] // 2
    first = values[..., :half]
    second = values[..., half:]
    cos_b = cosine[:, None, :]
    sin_b = sine[:, None, :] * sign
    return jnp.concatenate(
        [first * cos_b - second * sin_b, second * cos_b + first * sin_b], axis=-1
    )


def gelu_value(inner):
    return 0.5 * inner * (1.0 + lax.erf(inner * SQRT_HALF))


def gelu_slope(inner):
    return (
        0.5 * (1.0 + lax.erf(inner * SQRT_HALF))
        + inner * jnp.exp(-0.5 * inner * inner) * INV_SQRT_TAU
    )


def front_dot(left, right):
    return lax.dot_general(
        left, right, (((0,), (0,)), ((), ())), preferred_element_type=jnp.float32
    )


def back_dot(left, right):
    return lax.dot_general(
        left, right, (((1,), (1,)), ((), ())), preferred_element_type=jnp.float32
    )


def attend(queries, keys, values):
    total = keys.shape[0]
    step = math.gcd(total, 1024)
    rows, heads, width = queries.shape

    def measure(carry, index):
        top, mass = carry
        key_blk = lax.dynamic_slice_in_dim(keys, index * step, step, 0)
        score = (
            jnp.einsum("qhd,khd->hqk", queries, key_blk, preferred_element_type=jnp.float32) * 0.125
        )
        new_top = jnp.maximum(top, jnp.max(score, axis=-1))
        mass = mass * jnp.exp(top - new_top) + jnp.sum(jnp.exp(score - new_top[..., None]), axis=-1)
        return ((new_top, mass), None)

    start = (jnp.full((heads, rows), -jnp.inf, jnp.float32), jnp.zeros((heads, rows), jnp.float32))
    (top, mass), _ = lax.scan(measure, start, jnp.arange(total // step))
    lse = top + jnp.log(mass)

    def gather_values(acc, index):
        key_blk = lax.dynamic_slice_in_dim(keys, index * step, step, 0)
        val_blk = lax.dynamic_slice_in_dim(values, index * step, step, 0)
        score = (
            jnp.einsum("qhd,khd->hqk", queries, key_blk, preferred_element_type=jnp.float32) * 0.125
        )
        probs = jnp.exp(score - lse[..., None]).astype(jnp.bfloat16)
        return (
            acc + jnp.einsum("hqk,khd->hqd", probs, val_blk, preferred_element_type=jnp.float32),
            None,
        )

    acc, _ = lax.scan(
        gather_values, jnp.zeros((heads, rows, width), jnp.float32), jnp.arange(total // step)
    )
    result = acc.astype(jnp.bfloat16).transpose(1, 0, 2)
    return (result, lse)


def key_terms(queries, grads, lse, delta, key_blk, val_blk):
    score = jnp.einsum("qhd,khd->hqk", queries, key_blk, preferred_element_type=jnp.float32) * 0.125
    probs = jnp.exp(score - lse[..., None])
    d_probs = jnp.einsum("qhd,khd->hqk", grads, val_blk, preferred_element_type=jnp.float32)
    d_score = (probs * (d_probs - delta[..., None])).astype(jnp.bfloat16)
    d_key = jnp.einsum("hqk,qhd->khd", d_score, queries, preferred_element_type=jnp.float32) * 0.125
    d_value = jnp.einsum(
        "hqk,qhd->khd", probs.astype(jnp.bfloat16), grads, preferred_element_type=jnp.float32
    )
    return (d_key, d_value)


def attend_back(queries, keys, values, grads, lse, delta):
    total = keys.shape[0]
    step = math.gcd(total, 1024)
    rows, heads, width = queries.shape

    def attend_advance(d_query, index):
        key_blk = lax.dynamic_slice_in_dim(keys, index * step, step, 0)
        val_blk = lax.dynamic_slice_in_dim(values, index * step, step, 0)
        score = (
            jnp.einsum("qhd,khd->hqk", queries, key_blk, preferred_element_type=jnp.float32) * 0.125
        )
        probs = jnp.exp(score - lse[..., None])
        d_probs = jnp.einsum("qhd,khd->hqk", grads, val_blk, preferred_element_type=jnp.float32)
        d_score = (probs * (d_probs - delta[..., None])).astype(jnp.bfloat16)
        d_query = (
            d_query
            + jnp.einsum("hqk,khd->qhd", d_score, key_blk, preferred_element_type=jnp.float32)
            * 0.125
        )
        return (d_query, None)

    d_query, _ = lax.scan(
        attend_advance, jnp.zeros((rows, heads, width), jnp.float32), jnp.arange(total // step)
    )
    return d_query


def owner_fold(stats, own_keys, own_values):

    def fold(carry, piece, start):
        query_rows, grad_rows = piece
        count = query_rows.shape[0]
        step = math.gcd(count, 512)

        def fold_advance(acc, index):
            offset = index * step
            q_blk = lax.dynamic_slice_in_dim(query_rows, offset, step, 0)
            g_blk = lax.dynamic_slice_in_dim(grad_rows, offset, step, 0)
            lse_blk = lax.dynamic_slice_in_dim(stats[0], offset, step, 0)
            delta_blk = lax.dynamic_slice_in_dim(stats[1], offset, step, 0)
            d_key, d_value = key_terms(q_blk, g_blk, lse_blk.T, delta_blk.T, own_keys, own_values)
            return ((acc[0] + d_key, acc[1] + d_value), None)

        result, _ = lax.scan(fold_advance, carry, jnp.arange(count // step))
        return result

    return fold


def on_device(layer_input, gain_attn, w_qkv, w_out, gain_mlp, w_in, w_down, cotangent):
    whole = (
        lax.all_gather(gain_attn, "fsdp", axis=0, tiled=True),
        lax.all_gather(w_qkv, "fsdp", axis=0, tiled=True),
        lax.all_gather(w_out, "fsdp", axis=0, tiled=True),
        lax.all_gather(gain_mlp, "fsdp", axis=0, tiled=True),
        lax.all_gather(w_in, "fsdp", axis=0, tiled=True),
        lax.all_gather(w_down, "fsdp", axis=0, tiled=True),
    )
    gain_one = whole[0].astype(jnp.float32)
    qkv_full = whole[1]
    out_full = whole[2]
    gain_two = whole[3].astype(jnp.float32)
    in_full = whole[4]
    down_full = whole[5]
    rows, width = layer_input.shape
    groups = lax.axis_size("fsdp")
    block = rows * groups
    first_row = lax.axis_index("ctx") * block + lax.axis_index("fsdp") * rows
    xf = layer_input.astype(jnp.float32)
    xn1, n1, r1 = layer_norm(xf, gain_one)
    xn1b = xn1.astype(jnp.bfloat16)
    qkv = jnp.dot(xn1b, qkv_full, preferred_element_type=jnp.float32).reshape(rows, 3, H, HD)
    positions = (first_row + jnp.arange(rows)).astype(jnp.float32)
    cosine, sine = rope_tables(positions, HD)
    queries = rotate(qkv[:, 0], cosine, sine, 1.0).astype(jnp.bfloat16)
    keys = rotate(qkv[:, 1], cosine, sine, 1.0).astype(jnp.bfloat16)
    values = qkv[:, 2].astype(jnp.bfloat16)
    all_keys, all_values = (
        lax.all_gather(keys.reshape(rows, width), ("ctx", "fsdp"), axis=0, tiled=True),
        lax.all_gather(values.reshape(rows, width), ("ctx", "fsdp"), axis=0, tiled=True),
    )
    all_keys = all_keys.reshape(-1, H, HD)
    all_values = all_values.reshape(-1, H, HD)
    o_here, lse = attend(queries, all_keys, all_values)
    attended = o_here.reshape(rows, width)
    hidden = xf + jnp.dot(attended, out_full, preferred_element_type=jnp.float32)
    xn2, n2, r2 = layer_norm(hidden, gain_two)
    xn2b = xn2.astype(jnp.bfloat16)
    both = jnp.dot(xn2b, in_full, preferred_element_type=jnp.float32)
    ff_width = both.shape[1] // 2
    act_in = both[:, :ff_width]
    gate_in = both[:, ff_width:]
    mixed = (gelu_value(act_in) * gate_in).astype(jnp.bfloat16)
    output = (hidden + jnp.dot(mixed, down_full, preferred_element_type=jnp.float32)).astype(
        jnp.bfloat16
    )
    grad_f = cotangent.astype(jnp.float32)
    d_w_down = front_dot(mixed, cotangent)
    d_mixed = back_dot(cotangent, down_full)
    d_both = jnp.concatenate(
        [d_mixed * gate_in * gelu_slope(act_in), d_mixed * gelu_value(act_in)], axis=1
    ).astype(jnp.bfloat16)
    d_w_in = front_dot(xn2b, d_both)
    d_xn2 = back_dot(d_both, in_full)
    d_gain_mlp = jnp.sum(d_xn2 * n2, axis=0)
    d_hidden = grad_f + norm_back(d_xn2, n2, r2, gain_two)
    d_hidden_b = d_hidden.astype(jnp.bfloat16)
    d_w_out = front_dot(attended, d_hidden_b)
    d_attended = back_dot(d_hidden_b, out_full).astype(jnp.bfloat16)
    grads_here = d_attended.reshape(rows, H, HD)
    delta = jnp.sum(grads_here.astype(jnp.float32) * o_here.astype(jnp.float32), axis=-1).T
    d_query = attend_back(queries, all_keys, all_values, grads_here, lse, delta)
    stats = (
        lax.all_gather(lse.T, ("ctx", "fsdp"), axis=0, tiled=True),
        lax.all_gather(delta.T, ("ctx", "fsdp"), axis=0, tiled=True),
    )
    empty = jnp.zeros((rows, H, HD), jnp.float32)
    fold = owner_fold(stats, keys, values)
    d_key, d_value = fold(
        (empty, empty),
        (
            lax.all_gather(queries, ("ctx", "fsdp"), axis=0, tiled=True),
            lax.all_gather(grads_here, ("ctx", "fsdp"), axis=0, tiled=True),
        ),
        jnp.int32(0),
    )
    query_back = rotate(d_query, cosine, sine, -1.0).reshape(rows, width)
    key_back = rotate(d_key, cosine, sine, -1.0).reshape(rows, width)
    d_qkv = jnp.concatenate([query_back, key_back, d_value.reshape(rows, width)], axis=1).astype(
        jnp.bfloat16
    )
    d_w_qkv = front_dot(xn1b, d_qkv)
    d_xn1 = back_dot(d_qkv, qkv_full)
    d_gain_attn = jnp.sum(d_xn1 * n1, axis=0)
    d_x = d_hidden + norm_back(d_xn1, n1, r1, gain_one)
    shards = (
        lax.psum_scatter(
            d_gain_attn.astype(jnp.bfloat16), "fsdp", scatter_dimension=0, tiled=True
        ).astype(jnp.float32),
        lax.psum_scatter(
            d_w_qkv.astype(jnp.bfloat16), "fsdp", scatter_dimension=0, tiled=True
        ).astype(jnp.float32),
        lax.psum_scatter(
            d_w_out.astype(jnp.bfloat16), "fsdp", scatter_dimension=0, tiled=True
        ).astype(jnp.float32),
        lax.psum_scatter(
            d_gain_mlp.astype(jnp.bfloat16), "fsdp", scatter_dimension=0, tiled=True
        ).astype(jnp.float32),
        lax.psum_scatter(
            d_w_in.astype(jnp.bfloat16), "fsdp", scatter_dimension=0, tiled=True
        ).astype(jnp.float32),
        lax.psum_scatter(
            d_w_down.astype(jnp.bfloat16), "fsdp", scatter_dimension=0, tiled=True
        ).astype(jnp.float32),
    )
    summed = (
        lax.psum(shards[0].astype(jnp.bfloat16), "ctx").astype(jnp.float32),
        lax.psum(shards[1].astype(jnp.bfloat16), "ctx").astype(jnp.float32),
        lax.psum(shards[2].astype(jnp.bfloat16), "ctx").astype(jnp.float32),
        lax.psum(shards[3].astype(jnp.bfloat16), "ctx").astype(jnp.float32),
        lax.psum(shards[4].astype(jnp.bfloat16), "ctx").astype(jnp.float32),
        lax.psum(shards[5].astype(jnp.bfloat16), "ctx").astype(jnp.float32),
    )
    return (output, d_x, summed[0], summed[3], summed[1], summed[2], summed[4], summed[5])


def solution(mesh):
    return jax.shard_map(
        on_device,
        mesh=mesh,
        in_specs=(
            P(("ctx", "fsdp"), None),
            P("fsdp"),
            P("fsdp", None),
            P("fsdp", None),
            P("fsdp"),
            P("fsdp", None),
            P("fsdp", None),
            P(("ctx", "fsdp"), None),
        ),
        out_specs=(
            P(("ctx", "fsdp"), None),
            P(("ctx", "fsdp"), None),
            P("fsdp"),
            P("fsdp"),
            P("fsdp", None),
            P("fsdp", None),
            P("fsdp", None),
            P("fsdp", None),
        ),
        check_vma=False,
    )
```

profile of v0, /device:TPU:0, one launch (start us, length us, event | category | flops | bytes accessed | tf_op | source)
XLA Modules:
  0.0 1043.8 jit_solution(7189719437564355029)
XLA Ops:
  17.1 41.7 %all-gather.11.cloned.1.call-done = bf16[1024,3072]{1,0:T(8,128)(2,1)} async-done(((bf16[256,3072]{1,0:T(8,128)(2,1)}), bf16[1024,3072]{1,0:T(8,128)(2,1)}) %all-gather.11.cloned.1.call-update) | async-done | bytes 6291472 | tf_op jit(solution)/shard_map/all_gather | solution.py:176
  74.0 83.3 %all-gather.13.cloned.1.call-done = bf16[4096,1024]{0,1:T(8,128)(2,1)} async-done(((bf16[128,1024]{0,1:T(8,128)(2,1)}), bf16[4096,1024]{0,1:T(8,128)(2,1)}) %all-gather.13.cloned.1.call-update) | async-done | bytes 8388624 | tf_op jit(solution)/shard_map/all_gather | solution.py:202
  157.3 50.1 %while.48 = (s32[]{:T(128)}, f32[16,128]{1,0:T(8,128)S(1)}, f32[16,128]{1,0:T(8,128)S(1)}, s32[4]{0:T(128)S(1)}, bf16[4096,16,64]{0,2,1:T(8,128)(2,1)}, /*index=...) while((s32[]{:T(128)}, f32[16,128]{1,0:T(8,128)S(1)}, ...), condition=%wide.region_5.6_spmd.clone, body=%wide.region_2.5_spmd.clone.sunk | while | flops 278931456 | bytes 19243188 | solution.py:90
  207.4 43.3 %all-gather.15.cloned.1.call-done = bf16[4096,1024]{0,1:T(8,128)(2,1)} async-done(((bf16[128,1024]{0,1:T(8,128)(2,1)}), bf16[4096,1024]{0,1:T(8,128)(2,1)}) %all-gather.15.cloned.1.call-update) | async-done | bytes 8388624 | tf_op jit(solution)/shard_map/all_gather | solution.py:203
  250.7 25.5 %while.49 = (s32[]{:T(128)}, f32[16,128,64]{1,2,0:T(8,128)S(1)}, s32[4]{0:T(128)S(1)}, bf16[4096,16,64]{0,2,1:T(8,128)(2,1)}, bf16[128,16,64]{0,2,1:T(8,128)(2,1...) while((s32[]{:T(128)}, f32[16,128,64]{1,2,0:T(8,128)S(1)}, ...), condition=%wide.region_7.8_spmd.clone, body=%wide.region_6.7_spmd.clone.sunk | while | flops 543424512 | bytes 5514936 | solution.py:105
  278.6 67.3 %all-gather.19.cloned.1.call-done = bf16[1024,5248]{1,0:T(8,128)(2,1)} async-done(((bf16[256,5248]{1,0:T(8,128)(2,1)}), bf16[1024,5248]{1,0:T(8,128)(2,1)}) %all-gather.19.cloned.1.call-update) | async-done | bytes 10747920 | tf_op jit(solution)/shard_map/all_gather | solution.py:179
  346.0 7.3 fusion.107
  353.2 35.3 %all-gather.21.cloned.1.call-done = bf16[2624,1024]{1,0:T(8,128)(2,1)} async-done(((bf16[656,1024]{1,0:T(8,128)(2,1)}), bf16[2624,1024]{1,0:T(8,128)(2,1)}) %all-gather.21.cloned.1.call-update) | async-done | bytes 5373968 | tf_op jit(solution)/shard_map/all_gather | solution.py:180
  393.9 8.3 multiply_reduce_fusion
  422.3 42.8 %all_gather.45 = f32[4096,16]{0,1:T(8,128)S(1)} all-gather(f32[128,16]{0,1:T(8,128)S(1)} %bitcast.127), channel_id=1, replica_groups=mesh['ctx'=8,'fsdp'=4] {'ctx','fsdp'}, dimensions={0}, use_global_device_ids=true | all-gather | bytes 270336 | tf_op jit(solution)/shard_map/all_gather | solution.py:237
  465.3 38.5 %all_gather.47 = f32[4096,16]{0,1:T(8,128)S(1)} all-gather(f32[128,16]{0,1:T(8,128)S(1)} %multiply_reduce_fusion.1), channel_id=1, replica_groups=mesh['ctx'=8,'fsdp'=4] {'ctx','fsdp'}, dimensions={0}, use_global_device_ids=true | all-gather | bytes 270336 | tf_op jit(solution)/shard_map/all_gather | solution.py:238
  503.7 65.3 %while.50 = (s32[]{:T(128)}, f32[128,16,64]{0,2,1:T(8,128)}, s32[4]{0:T(128)S(1)}, bf16[4096,16,64]{0,2,1:T(8,128)(2,1)}, bf16[128,16,64]{0,2,1:T(8,128)(2,1)S(1...) while((s32[]{:T(128)}, f32[128,16,64]{0,2,1:T(8,128)}, ...), condition=%wide.region_14.15_spmd.clone, body=%wide.region_13.14_spmd.clone.sunk | while | flops 816185344 | bytes 24659660 | solution.py:145
  511.3 8.6 fusion.164
  527.4 8.6 fusion.164
  543.7 8.8 fusion.164
  560.0 9.0 fusion.164
  569.0 8.7 all-gather.25.cloned.1.call-done
  577.7 129.6 %while.51 = (s32[]{:T(128)}, f32[128,16,64]{0,2,1:T(8,128)}, f32[128,16,64]{0,2,1:T(8,128)S(1)}, s32[8]{0:T(128)S(1)}, bf16[4096,16,64]{0,2,1:T(8,128)(2,1)}, /*...) while((s32[]{:T(128)}, f32[128,16,64]{0,2,1:T(8,128)}, ...), condition=%wide.region_16.17_spmd.clone, body=%wide.region_15.16_spmd.clone.sunk | while | flops 545914880 | bytes 19629788 | solution.py:167
  631.1 7.6 fusion.173
  679.4 8.7 fusion.173
  713.6 40.5 %reduce-scatter.9.cloned.1.call-done = bf16[256,5248]{1,0:T(8,128)(2,1)} async-done(((bf16[1024,5248]{1,0:T(8,128)(2,1)}), bf16[256,5248]{1,0:T(8,128)(2,1)}) %reduce-scatter.9.cloned.1.call-update) | async-done | bytes 2686992 | tf_op jit(solution)/shard_map/reduce_scatter | solution.py:272
  754.0 61.3 %reduce-scatter.5.cloned.1.call-done = bf16[256,3072]{1,0:T(8,128)(2,1)} async-done(((bf16[1024,3072]{1,0:T(8,128)(2,1)}), bf16[256,3072]{1,0:T(8,128)(2,1)}) %reduce-scatter.5.cloned.1.call-update) | async-done | bytes 1572880 | tf_op jit(solution)/shard_map/reduce_scatter | solution.py:263
  833.7 22.5 %all-reduce.2 = (bf16[256]{0:T(256)(128)(2,1)S(1)}, bf16[256]{0:T(256)(128)(2,1)S(1)}) all-reduce(bf16[256]{0:T(256)(128)(2,1)S(1)} %dynamic-slice.1, bf16[256]{0:T(256)(128)(2,1)S(1)} %dynamic-slice.3), channel_id=1, replica_groups=mesh['ctx'=8,'fsdp'=4] {'ctx'}, use_global_device_ids=true, to_apply=%region_21.22 | all-reduce | flops 512 | bytes 2048 | tf_op jit(solution)/shard_map/psum | solution.py:280
  858.3 169.4 %all-reduce.7.cloned.1.call-done = (bf16[256,3072]{1,0:T(8,128)(2,1)}, bf16[256,1024]{1,0:T(8,128)(2,1)}, bf16[256,5248]{1,0:T(8,128)(2,1)}, bf16[656,1024]{1,0:T(8,128)(2,1)}) async-done(((bf16[256,3072]{1,0:T(8,128)(2,1)}, bf16[256,1024]{1,0:T(8,128)(2,1)}, bf16[256,5248]{1,0:T(8,128)(2,1)}, bf16[656,1024]{1,0:T(8,128)(2,1)}), (bf16[256,3072]{1,0:T(8,128)(2,1)}, bf16[256,1024]{1,0:T(8,128)(2,1)}, ...) | async-done | bytes 6127632 | tf_op jit(solution)/shard_map/psum | solution.py:281
  (206 shorter events, 293.5 us)
Async XLA Ops:
  7.2 51.6 %all-gather.11.cloned.1.call-start = ((), (), s32[]{:S(2)}) async-start(), calls=%async_computation.4 | async-start | bytes 7864320 | tf_op jit(solution)/shard_map/all_gather | solution.py:176
  7.9 149.4 %all-gather.13.cloned.1.call-start = ((), (), s32[]{:S(2)}) async-start(), calls=%async_computation.5 | async-start | bytes 8650752 | tf_op jit(solution)/shard_map/all_gather | solution.py:202
  65.4 185.3 %all-gather.15.cloned.1.call-start = ((), (), s32[]{:S(2)}) async-start(), calls=%async_computation.6 | async-start | bytes 8650752 | tf_op jit(solution)/shard_map/all_gather | solution.py:203
  66.2 210.0 %all-gather.17.cloned.1.call-start = ((), (), s32[]{:S(2)}) async-start(), calls=%async_computation.7 | async-start | bytes 2621440 | tf_op jit(solution)/shard_map/all_gather | solution.py:177
  66.8 279.2 %all-gather.19.cloned.1.call-start = ((), (), s32[]{:S(2)}) async-start(), calls=%async_computation.8 | async-start | bytes 13434880 | tf_op jit(solution)/shard_map/all_gather | solution.py:179
  67.4 321.2 %all-gather.21.cloned.1.call-start = ((), (), s32[]{:S(2)}) async-start(), calls=%async_computation.9 | async-start | bytes 6717440 | tf_op jit(solution)/shard_map/all_gather | solution.py:180
  68.0 501.0 %all-gather.23.cloned.1.call-start = ((), (), s32[]{:S(2)}) async-start(), calls=%async_computation.10 | async-start | bytes 8650752 | tf_op jit(solution)/shard_map/all_gather | solution.py:245
  68.9 508.8 %all-gather.25.cloned.1.call-start = ((), (), s32[]{:S(2)}) async-start(), calls=%async_computation.11 | async-start | bytes 8650752 | tf_op jit(solution)/shard_map/all_gather | solution.py:246
  250.7 25.6 %copy-start.2 = (bf16[128,1024]{1,0:T(8,128)(2,1)S(1)}, bf16[128,1024]{1,0:T(8,128)(2,1)}, u32[]{:S(2)}) copy-start(bf16[128,1024]{1,0:T(8,128)(2,1)} %param.16) | copy-start | bytes 786436
  346.0 42.6 %copy-start.8 = (bf16[128,1024]{1,0:T(8,128)(2,1)S(1)}, bf16[128,1024]{1,0:T(8,128)(2,1)}, u32[]{:S(2)}) copy-start(bf16[128,1024]{1,0:T(8,128)(2,1)} %param.23) | copy-start | bytes 786436
  393.9 8.3 copy-start.9
  393.9 8.3 copy-start.11
  393.9 8.6 copy-start.3
  404.2 309.3 %reduce-scatter.7.cloned.1.call-start = ((), (), s32[]{:S(2)}) async-start(), calls=%async_computation.13 | async-start | bytes 2621440 | tf_op jit(solution)/shard_map/reduce_scatter | solution.py:266
  406.3 307.3 %reduce-scatter.11.cloned.1.call-start = ((), (), s32[]{:S(2)}) async-start(), calls=%async_computation.15 | async-start | bytes 6717440 | tf_op jit(solution)/shard_map/reduce_scatter | solution.py:275
  412.3 341.7 %reduce-scatter.9.cloned.1.call-start = ((), (), s32[]{:S(2)}) async-start(), calls=%async_computation.14 | async-start | bytes 13434880 | tf_op jit(solution)/shard_map/reduce_scatter | solution.py:272
  420.4 44.8 %copy-start.6 = (bf16[128,1024]{0,1:T(8,128)(2,1)S(1)}, bf16[128,1024]{0,1:T(8,128)(2,1)}, u32[]{:S(2)}) copy-start(bf16[128,1024]{0,1:T(8,128)(2,1)} %copy.40) | copy-start | bytes 786436
  420.4 83.3 %copy-start = (bf16[128,16,64]{0,2,1:T(8,128)(2,1)S(1)}, bf16[128,16,64]{0,2,1:T(8,128)(2,1)}, u32[]{:S(2)}) copy-start(bf16[128,16,64]{0,2,1:T(8,128)(2,1)} %get-tuple-element.819) | copy-start | bytes 786436
  420.4 394.9 %reduce-scatter.5.cloned.1.call-start = ((), (), s32[]{:S(2)}) async-start(), calls=%async_computation.12 | async-start | bytes 7864320 | tf_op jit(solution)/shard_map/reduce_scatter | solution.py:263
  503.7 74.0 %copy-start.1 = (bf16[128,16,64]{0,2,1:T(8,128)(2,1)S(1)}, bf16[128,16,64]{0,2,1:T(8,128)(2,1)}, u32[]{:S(2)}) copy-start(bf16[128,16,64]{0,2,1:T(8,128)(2,1)} %maximum_convert_fusion) | copy-start | bytes 786436
  503.7 74.0 %copy-start.13 = (bf16[128,16,64]{0,2,1:T(8,128)(2,1)S(1)}, bf16[128,16,64]{0,2,1:T(8,128)(2,1)}, u32[]{:S(2)}) copy-start(bf16[128,16,64]{0,2,1:T(8,128)(2,1)} %slice_bitcast_fusion.2) | copy-start | bytes 786436
  713.3 314.5 %all-reduce.7.cloned.1.call-start = ((), (), s32[]{:S(2)}) async-start(), calls=%async_computation.16 | async-start | bytes 12255232 | tf_op jit(solution)/shard_map/psum | solution.py:281
  1027.8 3.6 copy-start.12
  1027.8 4.7 copy-start.5
  (5 other events, 9.8 us)
Sparse Core Ops, SparseCore 0:
  9.5 49.1 all-gather.10
  65.5 91.7 all-gather.12
  160.7 89.9 all-gather.14
  252.1 20.7 all-gather.16
  274.3 71.6 all-gather.18
  347.4 41.1 all-gather.20
  391.4 93.1 all-gather.22
  487.5 90.1 all-gather.24
  580.8 29.2 reduce-scatter.6
  613.1 52.1 reduce-scatter.10
  667.9 86.0 reduce-scatter.8
  756.4 58.8 reduce-scatter.4
  820.0 207.6 all-reduce.6
where the time goes:
time: 1050 us; the launch traced here: 1040 us
  waiting for transfers between devices  553 us (53%)
  matrix products  284 us (27%)
  blocking collectives  121 us (12%)
  other arithmetic  37.2 us (4%)
  local copies, waits for them, and re-layouts  18.6 us (2%)
  between operations  15.1 us (1%)
  loops' own time  13.9 us (1%)
    psum x1, waiting for transfers between devices, on_device(): lax.psum(shards[1].astype(jnp.bfloat16), 'ctx').astype(jnp.float32)  169 us
    all_gather x1, waiting for transfers between devices, on_device(): lax.all_gather(keys.reshape(rows, width), ('ctx', 'fsdp'), axis=0, tiled=...  83.3 us
    all_gather x1, waiting for transfers between devices, on_device(): lax.all_gather(w_in, 'fsdp', axis=0, tiled=True)  67.3 us
    reduce_scatter x1, waiting for transfers between devices, on_device(): lax.psum_scatter(d_w_qkv.astype(jnp.bfloat16), 'fsdp', scatter_dimension=...  61.3 us
    dot_general x8, matrix products, key_terms(): jnp.einsum('hqk,qhd->khd', d_score, queries, preferred_element_type=jnp.f...  57.2 us
    all_gather x1, waiting for transfers between devices, on_device(): lax.all_gather(values.reshape(rows, width), ('ctx', 'fsdp'), axis=0, tile...  43.3 us
    all_gather x1, blocking collectives, on_device(): lax.all_gather(lse.T, ('ctx', 'fsdp'), axis=0, tiled=True)  42.8 us
    all_gather x1, waiting for transfers between devices, on_device(): lax.all_gather(w_qkv, 'fsdp', axis=0, tiled=True)  41.7 us
  transfers between devices with their start and end apart: 13, of which 9 were waited for; matrix products, arithmetic and copies ran while one was open for 31% of the time, Pallas kernels for 0%

commit v1 on v0

--- a/solution.py
+++ b/solution.py
@@ -278,7 +278,7 @@
     )
     summed = (
         lax.psum(shards[0].astype(jnp.bfloat16), "ctx").astype(jnp.float32),
-        lax.psum(shards[1].astype(jnp.bfloat16), "ctx").astype(jnp.float32),
+        jnp.sum(lax.all_gather(shards[1].astype(jnp.bfloat16), "ctx"), axis=0).astype(jnp.float32),
         lax.psum(shards[2].astype(jnp.bfloat16), "ctx").astype(jnp.float32),
         lax.psum(shards[3].astype(jnp.bfloat16), "ctx").astype(jnp.float32),
         lax.psum(shards[4].astype(jnp.bfloat16), "ctx").astype(jnp.float32),

time: 1050 us -> 1190 us (1.13)
  waiting for transfers between devices: 553 us -> 680 us
    all_gather x0 -> x1, waiting for transfers between devices: none -> 169 us  [on_device(): lax.all_gather(shards[1].astype(jnp.bfloat16), 'ctx')]
    psum x1, waiting for transfers between devices: 169 us -> 128 us  [on_device(): lax.psum(shards[2].astype(jnp.bfloat16), 'ctx').astype(jnp.float32)]
  transfers between devices with their start and end apart: 13 -> 14, of which waited for: 9 -> 10; matrix products, arithmetic and copies ran while one was open for 31% -> 28% of each run, Pallas kernels for 0% -> 0%
where the time goes in v1:
time: 1190 us; the launch traced here: 1180 us
  waiting for transfers between devices  680 us (57%)
  matrix products  284 us (24%)
  blocking collectives  121 us (10%)
  other arithmetic  45.8 us (4%)
  local copies, waits for them, and re-layouts  18 us (2%)
  between operations  15.2 us (1%)
  loops' own time  14.1 us (1%)
    all_gather x1, waiting for transfers between devices, on_device(): lax.all_gather(shards[1].astype(jnp.bfloat16), 'ctx')  169 us
    psum x1, waiting for transfers between devices, on_device(): lax.psum(shards[2].astype(jnp.bfloat16), 'ctx').astype(jnp.float32)  128 us
    all_gather x1, waiting for transfers between devices, on_device(): lax.all_gather(keys.reshape(rows, width), ('ctx', 'fsdp'), axis=0, tiled=...  83.3 us
    all_gather x1, waiting for transfers between devices, on_device(): lax.all_gather(w_in, 'fsdp', axis=0, tiled=True)  67.3 us
    reduce_scatter x1, waiting for transfers between devices, on_device(): lax.psum_scatter(d_w_qkv.astype(jnp.bfloat16), 'fsdp', scatter_dimension=...  61 us
    dot_general x8, matrix products, key_terms(): jnp.einsum('hqk,qhd->khd', d_score, queries, preferred_element_type=jnp.f...  57.2 us
    all_gather x1, waiting for transfers between devices, on_device(): lax.all_gather(values.reshape(rows, width), ('ctx', 'fsdp'), axis=0, tile...  43.2 us
    all_gather x1, blocking collectives, on_device(): lax.all_gather(lse.T, ('ctx', 'fsdp'), axis=0, tiled=True)  42.8 us
  transfers between devices with their start and end apart: 14, of which 10 were waited for; matrix products, arithmetic and copies ran while one was open for 28% of the time, Pallas kernels for 0%

profile of v1, /device:TPU:0, one launch (start us, length us, event | category | flops | bytes accessed | tf_op | source)
XLA Modules:
  0.0 1178.8 jit_solution(15846477218426016681)
XLA Ops:
  17.1 41.7 %all-gather.13.cloned.1.call-done = bf16[1024,3072]{1,0:T(8,128)(2,1)} async-done(((bf16[256,3072]{1,0:T(8,128)(2,1)}), bf16[1024,3072]{1,0:T(8,128)(2,1)}) %all-gather.13.cloned.1.call-update) | async-done | bytes 6291472 | tf_op jit(solution)/shard_map/all_gather | solution.py:176
  74.0 83.3 %all-gather.15.cloned.1.call-done = bf16[4096,1024]{0,1:T(8,128)(2,1)} async-done(((bf16[128,1024]{0,1:T(8,128)(2,1)}), bf16[4096,1024]{0,1:T(8,128)(2,1)}) %all-gather.15.cloned.1.call-update) | async-done | bytes 8388624 | tf_op jit(solution)/shard_map/all_gather | solution.py:202
  157.3 50.2 %while.48 = (s32[]{:T(128)}, f32[16,128]{1,0:T(8,128)S(1)}, f32[16,128]{1,0:T(8,128)S(1)}, s32[4]{0:T(128)S(1)}, bf16[4096,16,64]{0,2,1:T(8,128)(2,1)}, /*index=...) while((s32[]{:T(128)}, f32[16,128]{1,0:T(8,128)S(1)}, ...), condition=%wide.region_5.6_spmd.clone, body=%wide.region_2.5_spmd.clone.sunk | while | flops 278931456 | bytes 19243188 | solution.py:90
  207.5 43.2 %all-gather.17.cloned.1.call-done = bf16[4096,1024]{0,1:T(8,128)(2,1)} async-done(((bf16[128,1024]{0,1:T(8,128)(2,1)}), bf16[4096,1024]{0,1:T(8,128)(2,1)}) %all-gather.17.cloned.1.call-update) | async-done | bytes 8388624 | tf_op jit(solution)/shard_map/all_gather | solution.py:203
  250.7 25.5 %while.49 = (s32[]{:T(128)}, f32[16,128,64]{1,2,0:T(8,128)S(1)}, s32[4]{0:T(128)S(1)}, bf16[4096,16,64]{0,2,1:T(8,128)(2,1)}, bf16[128,16,64]{0,2,1:T(8,128)(2,1...) while((s32[]{:T(128)}, f32[16,128,64]{1,2,0:T(8,128)S(1)}, ...), condition=%wide.region_7.8_spmd.clone, body=%wide.region_6.7_spmd.clone.sunk | while | flops 543424512 | bytes 5514936 | solution.py:105
  278.6 67.3 %all-gather.21.cloned.1.call-done = bf16[1024,5248]{1,0:T(8,128)(2,1)} async-done(((bf16[256,5248]{1,0:T(8,128)(2,1)}), bf16[1024,5248]{1,0:T(8,128)(2,1)}) %all-gather.21.cloned.1.call-update) | async-done | bytes 10747920 | tf_op jit(solution)/shard_map/all_gather | solution.py:179
  353.2 35.3 %all-gather.23.cloned.1.call-done = bf16[2624,1024]{1,0:T(8,128)(2,1)} async-done(((bf16[656,1024]{1,0:T(8,128)(2,1)}), bf16[2624,1024]{1,0:T(8,128)(2,1)}) %all-gather.23.cloned.1.call-update) | async-done | bytes 5373968 | tf_op jit(solution)/shard_map/all_gather | solution.py:180
  393.9 8.3 multiply_reduce_fusion
  422.3 42.8 %all_gather.51 = f32[4096,16]{0,1:T(8,128)S(1)} all-gather(f32[128,16]{0,1:T(8,128)S(1)} %bitcast.129), channel_id=1, replica_groups=mesh['ctx'=8,'fsdp'=4] {'ctx','fsdp'}, dimensions={0}, use_global_device_ids=true | all-gather | bytes 270336 | tf_op jit(solution)/shard_map/all_gather | solution.py:237
  465.2 38.5 %all_gather.53 = f32[4096,16]{0,1:T(8,128)S(1)} all-gather(f32[128,16]{0,1:T(8,128)S(1)} %multiply_reduce_fusion.1), channel_id=1, replica_groups=mesh['ctx'=8,'fsdp'=4] {'ctx','fsdp'}, dimensions={0}, use_global_device_ids=true | all-gather | bytes 270336 | tf_op jit(solution)/shard_map/all_gather | solution.py:238
  503.7 65.5 %while.50 = (s32[]{:T(128)}, f32[128,16,64]{0,2,1:T(8,128)}, s32[4]{0:T(128)S(1)}, bf16[4096,16,64]{0,2,1:T(8,128)(2,1)}, bf16[128,16,64]{0,2,1:T(8,128)(2,1)S(1...) while((s32[]{:T(128)}, f32[128,16,64]{0,2,1:T(8,128)}, ...), condition=%wide.region_14.15_spmd.clone, body=%wide.region_13.14_spmd.clone.sunk | while | flops 816185344 | bytes 24659660 | solution.py:145
  511.3 8.6 fusion.164
  527.5 8.7 fusion.164
  543.9 8.8 fusion.164
  560.3 8.9 fusion.164
  569.2 8.5 all-gather.27.cloned.1.call-done
  577.7 129.5 %while.51 = (s32[]{:T(128)}, f32[128,16,64]{0,2,1:T(8,128)}, f32[128,16,64]{0,2,1:T(8,128)S(1)}, s32[8]{0:T(128)S(1)}, bf16[4096,16,64]{0,2,1:T(8,128)(2,1)}, /*...) while((s32[]{:T(128)}, f32[128,16,64]{0,2,1:T(8,128)}, ...), condition=%wide.region_16.17_spmd.clone, body=%wide.region_15.16_spmd.clone.sunk | while | flops 545914880 | bytes 19629788 | solution.py:167
  631.1 7.6 fusion.173
  679.3 8.8 fusion.173
  713.4 40.7 %reduce-scatter.9.cloned.1.call-done = bf16[256,5248]{1,0:T(8,128)(2,1)} async-done(((bf16[1024,5248]{1,0:T(8,128)(2,1)}), bf16[256,5248]{1,0:T(8,128)(2,1)}) %reduce-scatter.9.cloned.1.call-update) | async-done | bytes 2686992 | tf_op jit(solution)/shard_map/reduce_scatter | solution.py:272
  754.3 61.0 %reduce-scatter.5.cloned.1.call-done = bf16[256,3072]{1,0:T(8,128)(2,1)} async-done(((bf16[1024,3072]{1,0:T(8,128)(2,1)}), bf16[256,3072]{1,0:T(8,128)(2,1)}) %reduce-scatter.5.cloned.1.call-update) | async-done | bytes 1572880 | tf_op jit(solution)/shard_map/reduce_scatter | solution.py:263
  833.1 22.7 %all-reduce.2 = (bf16[256]{0:T(256)(128)(2,1)S(1)}, bf16[256]{0:T(256)(128)(2,1)S(1)}) all-reduce(bf16[256]{0:T(256)(128)(2,1)S(1)} %dynamic-slice.1, bf16[256]{0:T(256)(128)(2,1)S(1)} %dynamic-slice.3), channel_id=1, replica_groups=mesh['ctx'=8,'fsdp'=4] {'ctx'}, use_global_device_ids=true, to_apply=%region_21.22 | all-reduce | flops 512 | bytes 2048 | tf_op jit(solution)/shard_map/psum | solution.py:280
  858.0 127.5 %all-reduce.7.cloned.1.call-done = (bf16[256,1024]{1,0:T(8,128)(2,1)}, bf16[256,5248]{1,0:T(8,128)(2,1)}, bf16[656,1024]{1,0:T(8,128)(2,1)}) async-done(((bf16[256,1024]{1,0:T(8,128)(2,1)}, bf16[256,5248]{1,0:T(8,128)(2,1)}, bf16[656,1024]{1,0:T(8,128)(2,1)}), (bf16[256,1024]{1,0:T(8,128)(2,1)}, bf16[256,5248]{1,0:T(8,128)(2,1)}, bf16[656,1024]{1,0:T(8,128)(2,1)})) %all-reduce.7.cloned.1.call-update) | async-done | bytes 4554768 | tf_op jit(solution)/shard_map/psum | solution.py:282
  994.1 168.6 %all-gather.29.cloned.1.call-done = bf16[2048,3072]{1,0:T(8,128)(2,1)} async-done(((bf16[256,3072]{1,0:T(8,128)(2,1)}), bf16[2048,3072]{1,0:T(8,128)(2,1)}) %all-gather.29.cloned.1.call-update) | async-done | bytes 12582928 | tf_op jit(solution)/shard_map/all_gather | solution.py:281
  (206 shorter events, 308.7 us)
Async XLA Ops:
  7.2 51.6 %all-gather.13.cloned.1.call-start = ((), (), s32[]{:S(2)}) async-start(), calls=%async_computation.4 | async-start | bytes 7864320 | tf_op jit(solution)/shard_map/all_gather | solution.py:176
  7.9 149.4 %all-gather.15.cloned.1.call-start = ((), (), s32[]{:S(2)}) async-start(), calls=%async_computation.5 | async-start | bytes 8650752 | tf_op jit(solution)/shard_map/all_gather | solution.py:202
  65.4 185.3 %all-gather.17.cloned.1.call-start = ((), (), s32[]{:S(2)}) async-start(), calls=%async_computation.6 | async-start | bytes 8650752 | tf_op jit(solution)/shard_map/all_gather | solution.py:203
  66.2 210.0 %all-gather.19.cloned.1.call-start = ((), (), s32[]{:S(2)}) async-start(), calls=%async_computation.7 | async-start | bytes 2621440 | tf_op jit(solution)/shard_map/all_gather | solution.py:177
  66.8 279.2 %all-gather.21.cloned.1.call-start = ((), (), s32[]{:S(2)}) async-start(), calls=%async_computation.8 | async-start | bytes 13434880 | tf_op jit(solution)/shard_map/all_gather | solution.py:179
  67.4 321.2 %all-gather.23.cloned.1.call-start = ((), (), s32[]{:S(2)}) async-start(), calls=%async_computation.9 | async-start | bytes 6717440 | tf_op jit(solution)/shard_map/all_gather | solution.py:180
  68.0 501.2 %all-gather.25.cloned.1.call-start = ((), (), s32[]{:S(2)}) async-start(), calls=%async_computation.10 | async-start | bytes 8650752 | tf_op jit(solution)/shard_map/all_gather | solution.py:245
  68.9 508.9 %all-gather.27.cloned.1.call-start = ((), (), s32[]{:S(2)}) async-start(), calls=%async_computation.11 | async-start | bytes 8650752 | tf_op jit(solution)/shard_map/all_gather | solution.py:246
  250.7 25.6 %copy-start.2 = (bf16[128,1024]{1,0:T(8,128)(2,1)S(1)}, bf16[128,1024]{1,0:T(8,128)(2,1)}, u32[]{:S(2)}) copy-start(bf16[128,1024]{1,0:T(8,128)(2,1)} %param.16) | copy-start | bytes 786436
  346.0 42.6 %copy-start.7 = (bf16[128,1024]{1,0:T(8,128)(2,1)S(1)}, bf16[128,1024]{1,0:T(8,128)(2,1)}, u32[]{:S(2)}) copy-start(bf16[128,1024]{1,0:T(8,128)(2,1)} %param.23) | copy-start | bytes 786436
  393.9 8.3 copy-start.8
  393.9 8.3 copy-start.10
  393.9 8.6 copy-start.3
  404.2 309.1 %reduce-scatter.7.cloned.1.call-start = ((), (), s32[]{:S(2)}) async-start(), calls=%async_computation.13 | async-start | bytes 2621440 | tf_op jit(solution)/shard_map/reduce_scatter | solution.py:266
  406.3 307.1 %reduce-scatter.11.cloned.1.call-start = ((), (), s32[]{:S(2)}) async-start(), calls=%async_computation.15 | async-start | bytes 6717440 | tf_op jit(solution)/shard_map/reduce_scatter | solution.py:275
  412.3 341.7 %reduce-scatter.9.cloned.1.call-start = ((), (), s32[]{:S(2)}) async-start(), calls=%async_computation.14 | async-start | bytes 13434880 | tf_op jit(solution)/shard_map/reduce_scatter | solution.py:272
  420.4 44.8 %copy-start.5 = (bf16[128,1024]{0,1:T(8,128)(2,1)S(1)}, bf16[128,1024]{0,1:T(8,128)(2,1)}, u32[]{:S(2)}) copy-start(bf16[128,1024]{0,1:T(8,128)(2,1)} %copy.40) | copy-start | bytes 786436
  420.4 83.3 %copy-start = (bf16[128,16,64]{0,2,1:T(8,128)(2,1)S(1)}, bf16[128,16,64]{0,2,1:T(8,128)(2,1)}, u32[]{:S(2)}) copy-start(bf16[128,16,64]{0,2,1:T(8,128)(2,1)} %get-tuple-element.817) | copy-start | bytes 786436
  420.4 394.9 %reduce-scatter.5.cloned.1.call-start = ((), (), s32[]{:S(2)}) async-start(), calls=%async_computation.12 | async-start | bytes 7864320 | tf_op jit(solution)/shard_map/reduce_scatter | solution.py:263
  503.7 74.0 %copy-start.1 = (bf16[128,16,64]{0,2,1:T(8,128)(2,1)S(1)}, bf16[128,16,64]{0,2,1:T(8,128)(2,1)}, u32[]{:S(2)}) copy-start(bf16[128,16,64]{0,2,1:T(8,128)(2,1)} %maximum_convert_fusion) | copy-start | bytes 786436
  503.7 74.0 %copy-start.11 = (bf16[128,16,64]{0,2,1:T(8,128)(2,1)S(1)}, bf16[128,16,64]{0,2,1:T(8,128)(2,1)}, u32[]{:S(2)}) copy-start(bf16[128,16,64]{0,2,1:T(8,128)(2,1)} %slice_bitcast_fusion.2) | copy-start | bytes 786436
  713.3 272.2 %all-reduce.7.cloned.1.call-start = ((), (), s32[]{:S(2)}) async-start(), calls=%async_computation.17 | async-start | bytes 9109504 | tf_op jit(solution)/shard_map/psum | solution.py:282
  754.0 61.3 %copy-start.13 = (u32[32]{0:T(128)S(1)}, u32[32]{0:T(128)}, u32[]{:S(2)}) copy-start(u32[32]{0:T(128)} %constant.115) | copy-start | bytes 388
  754.1 408.6 %all-gather.29.cloned.1.call-start = ((), (), s32[]{:S(2)}) async-start(), calls=%async_computation.16 | async-start | bytes 14155776 | tf_op jit(solution)/shard_map/all_gather | solution.py:281
  (4 other events, 11.0 us)
Sparse Core Ops, SparseCore 0:
  9.5 49.1 all-gather.12
  65.5 91.7 all-gather.14
  160.7 89.9 all-gather.16
  252.1 20.7 all-gather.18
  274.3 71.6 all-gather.20
  347.4 41.1 all-gather.22
  391.4 93.1 all-gather.24
  487.4 90.2 all-gather.26
  580.8 29.2 reduce-scatter.6
  613.2 52.1 reduce-scatter.10
  668.0 85.9 reduce-scatter.8
  756.4 58.8 reduce-scatter.4
  819.3 166.1 all-reduce.6
  987.6 175.1 all-gather.28
